TPU v7x, 512 devices: a whole 4x8x8 slice. The times are simulated.
512 devices in a mesh: ev: 32 (over x, y_lo, core), ch: 16 (over y_hi, z).
Axes of the slice: x: 4, y: 8 (y_hi: 2, y_lo: 4; y = y_hi * 4 + y_lo), z: 8, core: 2. Of those that a mesh axis runs over, the one named last changes fastest.
Arguments:
- spectra: float32 [512, 16, 65536], P('ev', None, 'ch'), as said below
- tile_mask: int32 [512, 512], P('ev', 'ch'), may hold values 0 or 1
- source_init: float32 [512, 16], P('ev'), may hold values from -6 to 6
- site_init: float32 [16, 65536], P(None, 'ch'), may hold values from -6 to 6
- event_pos: float32 [3, 512], P(None, 'ev'), may hold values from 5 to 50
- channel_pos: float32 [2, 65536], P(None, 'ch'), may hold values from 0 to 50
- atten: float32 [16], replicated, may hold values from 0.02 to 0.3
Outputs:
- source: float32 [512, 16], P('ev')
- site: float32 [16, 65536], P(None, 'ch')
Inputs may be any that keep to these rules, and one draw needn't show every extreme that they name: spectra are log amplitudes of order one to a few, with outliers. `tile_mask`: 0 marks an event invalid on a whole tile of 128 channels.
All inputs are finite; a program needn't handle non-finite values. No bound on the sum of `tile_mask` on one device may be relied on, other than what follows from the above.
Results may differ from a plain program's by a relative error of at most 0.0001.
Values sent between devices are 32-bit elements; how exact they have to be, the bound alone decides.
A program may use at most 64 MiB of HBM per device.

v0:
```python
import jax
import jax.numpy as jnp
from jax import lax
from jax.sharding import PartitionSpec as P

ITERS = 2


def on_device(spectra, tile_mask, source_init, site_init, event_pos, channel_pos, atten):
    ev_n, freqs, ch_n = spectra.shape
    total_ch = ch_n * lax.axis_size("ch")
    valid = jnp.repeat(tile_mask, 128, axis=1).astype(jnp.float32)[:, None, :]
    count_part = jnp.sum(valid)
    east = event_pos[0][:, None] - channel_pos[0][None, :]
    north = event_pos[1][:, None] - channel_pos[1][None, :]
    depth = event_pos[2][:, None]
    travel = jnp.sqrt(east * east + north * north + depth * depth) / 3.0
    path = atten[None, :, None] * travel[:, None, :]
    source = source_init
    site = site_init
    for step in range(ITERS):
        resid = spectra - source[:, :, None] - site[None, :, :] + path
        abs_part = jnp.sum(valid * jnp.abs(resid), axis=(0, 2))
        absum, count = lax.psum((abs_part, count_part), ("ev", "ch"))
        delta = 1.345 * (1.2533 * absum / jnp.maximum(count, 1.0) + 1e-05)
        limit = delta[None, :, None]
        weight = limit / jnp.maximum(jnp.abs(resid), limit) * valid
        product = weight * resid
        src_num, src_den = lax.psum((jnp.sum(product, axis=2), jnp.sum(weight, axis=2)), "ch")
        site_num = jnp.sum(product, axis=0)
        site_den = jnp.sum(weight, axis=0)
        site_num, site_den = lax.psum((site_num, site_den), "ev")
        site = site + 0.5 * site_num / (site_den + 1.0)
        source = source + 0.5 * src_num / (src_den + 1.0)
        shift = lax.psum(jnp.sum(site, axis=1), "ch") / total_ch
        site = site - shift[:, None]
        source = source + shift[None, :]
    return (source, site)


def solution(mesh):
    in_specs = (
        P("ev", None, "ch"),
        P("ev", "ch"),
        P("ev", None),
        P(None, "ch"),
        P(None, "ev"),
        P(None, "ch"),
        P(),
    )
    out_specs = (P("ev", None), P(None, "ch"))
    return jax.shard_map(
        on_device, mesh=mesh, in_specs=in_specs, out_specs=out_specs, check_vma=False
    )
```

profile of v0, /device:TPU:8, one launch (start us, length us, event | category | flops | bytes accessed | tf_op | source)
XLA Modules:
  0.0 981.2 jit_solution(700504949465934503)
XLA Ops:
  7.2 0.0 copy-start.2
  7.2 0.0 copy-start
  7.2 0.0 copy-start.1
  7.2 0.0 all-reduce.10.cloned.1.call-start
  7.2 0.8 slice_bitcast_fusion.1
  8.0 0.7 convert_element_type.13
  8.7 0.9 fusion.8
  9.6 0.1 broadcast_in_dim.2
  9.7 0.2 copy.11
  9.9 0.2 sqrt_multiply_fusion
  10.1 3.4 multiply_reduce_fusion.1
  13.5 0.7 broadcast_reduce_fusion
  14.2 104.9 %all-reduce = (f32[16]{0:T(128)S(1)}, f32[]{:T(128)}) all-reduce(f32[16]{0:T(128)S(1)} %multiply_reduce_fusion.1, f32[]{:T(128)} %broadcast_reduce_fusion), channel_id=1, replica_groups=mesh['ev'=32,'ch'=16] {'ev','ch'}, use_global_device_ids=true, to_apply=%region_1.0 | all-reduce | flops 17 | bytes 136 | tf_op jit(solution)/shard_map/psum | solution.py:24
  119.7 0.0 copy-done.2
  119.8 0.0 copy-done
  119.8 0.0 copy-done.1
  119.8 5.4 fusion.4
  125.1 0.0 all-reduce.10.cloned.1.call-update
  125.2 0.0 all-reduce.8.cloned.1.call-start
  125.2 271.7 %all-reduce.10.cloned.1.call-done = (f32[16,4096]{1,0:T(8,128)}, f32[16,4096]{1,0:T(8,128)}) async-done(((f32[16,4096]{1,0:T(8,128)}, f32[16,4096]{1,0:T(8,128)}), (f32[16,4096]{1,0:T(8,128)}, f32[16,4096]{1,0:T(8,128)})) %all-reduce.10.cloned.1.call-update) | async-done | bytes 524304 | tf_op jit(solution)/shard_map/psum | solution.py:32
  397.0 1.2 fusion.7
  398.2 98.8 %all-reduce.4 = (f32[16,16]{1,0:T(8,128)S(1)}, f32[16,16]{1,0:T(8,128)S(1)}, f32[16]{0:T(128)S(1)}) all-reduce(f32[16,16]{1,0:T(8,128)S(1)} %get-tuple-element.9, f32[16,16]{1,0:T(8,128)S(1)} %get-tuple-element.5, f32[16]{0:T(128)S(1)} %get-tuple-element.24), channel_id=1, replica_groups=mesh['ev'=32,'ch'=16] {'ch'}, use_global_device_ids=true, to_apply=%region_7.0 | all-reduce | flops 528 | bytes 4224 | tf_op jit(solution)/shard_map/psum | solution.py:29
  497.0 0.1 broadcast_subtract_fusion.1
  497.1 3.3 multiply_reduce_fusion
  500.4 97.2 %psum.101 = f32[16]{0:T(128)S(1)} all-reduce(f32[16]{0:T(128)S(1)} %multiply_reduce_fusion), channel_id=1, replica_groups=mesh['ev'=32,'ch'=16] {'ev','ch'}, use_global_device_ids=true, to_apply=%region_15.0 | all-reduce | flops 16 | bytes 128 | tf_op jit(solution)/shard_map/psum | solution.py:24
  597.6 5.4 fusion.2
  602.9 0.0 all-reduce.8.cloned.1.call-update
  603.0 270.0 %all-reduce.8.cloned.1.call-done = (f32[16,4096]{1,0:T(8,128)}, f32[16,4096]{1,0:T(8,128)}) async-done(((f32[16,4096]{1,0:T(8,128)}, f32[16,4096]{1,0:T(8,128)}), (f32[16,4096]{1,0:T(8,128)}, f32[16,4096]{1,0:T(8,128)})) %all-reduce.8.cloned.1.call-update) | async-done | bytes 524304 | tf_op jit(solution)/shard_map/psum | solution.py:32
  872.9 1.2 fusion.6
  874.2 98.8 %all-reduce.3 = (f32[16,16]{1,0:T(8,128)S(1)}, f32[16,16]{1,0:T(8,128)S(1)}, f32[16]{0:T(128)S(1)}) all-reduce(f32[16,16]{1,0:T(8,128)S(1)} %get-tuple-element.7, f32[16,16]{1,0:T(8,128)S(1)} %get-tuple-element.3, f32[16]{0:T(128)S(1)} %get-tuple-element.22), channel_id=1, replica_groups=mesh['ev'=32,'ch'=16] {'ch'}, use_global_device_ids=true, to_apply=%region_19.0 | all-reduce | flops 528 | bytes 4224 | tf_op jit(solution)/shard_map/psum | solution.py:29
  973.0 0.8 broadcast_subtract_fusion
  973.8 0.6 add_add_fusion
  (5 shorter events, 0.0 us)
Async XLA Ops:
  7.2 112.6 %copy-start.2 = (f32[16]{0:T(128)S(1)}, f32[16]{0:T(128)}, u32[]{:S(2)}) copy-start(f32[16]{0:T(128)} %param.13) | copy-start | bytes 196
  7.2 112.6 %copy-start = (f32[16,4096]{1,0:T(8,128)S(1)}, f32[16,4096]{1,0:T(8,128)}, u32[]{:S(2)}) copy-start(f32[16,4096]{1,0:T(8,128)} %param.10) | copy-start | bytes 786436
  7.2 112.6 %copy-start.1 = (f32[16,16]{1,0:T(8,128)S(1)}, f32[16,16]{1,0:T(8,128)}, u32[]{:S(2)}) copy-start(f32[16,16]{1,0:T(8,128)} %param.9) | copy-start | bytes 3076
  7.2 389.8 %all-reduce.10.cloned.1.call-start = ((), (), s32[]{:S(2)}) async-start(), calls=%async_computation.1 | async-start | bytes 1048576 | tf_op jit(solution)/shard_map/psum | solution.py:32
  125.2 747.8 %all-reduce.8.cloned.1.call-start = ((), (), s32[]{:S(2)}) async-start(), calls=%async_computation | async-start | bytes 1048576 | tf_op jit(solution)/shard_map/psum | solution.py:32
Sparse Core Ops, SparseCore 0:
  125.3 271.6 all-reduce.9
  603.1 269.8 all-reduce.7
where the time goes:
time: 982 us; the launch traced here: 981 us
  waiting for transfers between devices  542 us (55%)
  blocking collectives  400 us (41%)
  other arithmetic  23.8 us (2%)
  between operations  14.8 us (2%)
    psum x2, waiting for transfers between devices, on_device(): site_num, site_den = lax.psum((site_num, site_den), 'ev')  542 us
    psum x2, blocking collectives, on_device(): absum, count = lax.psum((abs_part, count_part), ('ev', 'ch'))  202 us
    psum x2, blocking collectives, on_device(): lax.psum((jnp.sum(product, axis=2), jnp.sum(weight, axis=2)), 'ch')  198 us
  transfers between devices with their start and end apart: 2, of which 2 were waited for; matrix products, arithmetic and copies ran while one was open for 0% of the time, Pallas kernels for 0%

commit v1 on v0

--- a/solution.py
+++ b/solution.py
@@ -4,6 +4,12 @@
 from jax.sharding import PartitionSpec as P
 
 ITERS = 2
+
+
+def try_all_patch(a0):
+    for u in ("ev", "ch"):
+        a0 = lax.psum(a0, u)
+    return a0
 
 
 def on_device(spectra, tile_mask, source_init, site_init, event_pos, channel_pos, atten):
@@ -21,7 +27,7 @@
     for step in range(ITERS):
         resid = spectra - source[:, :, None] - site[None, :, :] + path
         abs_part = jnp.sum(valid * jnp.abs(resid), axis=(0, 2))
-        absum, count = lax.psum((abs_part, count_part), ("ev", "ch"))
+        absum, count = try_all_patch((abs_part, count_part))
         delta = 1.345 * (1.2533 * absum / jnp.maximum(count, 1.0) + 1e-05)
         limit = delta[None, :, None]
         weight = limit / jnp.maximum(jnp.abs(resid), limit) * valid

time: 982 us -> 1020 us (1.039)
  blocking collectives: 400 us -> 436 us
    psum x2 -> x4, blocking collectives: 202 us -> 239 us  [try_all_patch(): a0 = lax.psum(a0, u)]
where the time goes in v1:
time: 1020 us
  waiting for transfers between devices  547 us (54%)
  blocking collectives  436 us (43%)
  other arithmetic  23.8 us (2%)
  between operations  14.8 us (1%)
    psum x2, waiting for transfers between devices, on_device(): site_num, site_den = lax.psum((site_num, site_den), 'ev')  547 us
    psum x4, blocking collectives, try_all_patch(): a0 = lax.psum(a0, u)  239 us
    psum x2, blocking collectives, on_device(): lax.psum((jnp.sum(product, axis=2), jnp.sum(weight, axis=2)), 'ch')  198 us
  transfers between devices with their start and end apart: 2, of which 2 were waited for; matrix products, arithmetic and copies ran while one was open for 0% of the time, Pallas kernels for 0%

profile of v1, /device:TPU:8, one launch (start us, length us, event | category | flops | bytes accessed | tf_op | source)
XLA Modules:
  0.0 1023.1 jit_solution(6069354510742669470)
XLA Ops:
  7.2 0.0 copy-start.2
  7.2 0.0 copy-start
  7.2 0.0 copy-start.1
  7.2 0.0 all-reduce.11.cloned.1.call-start
  7.2 0.8 slice_bitcast_fusion.1
  8.0 0.7 convert_element_type.13
  8.7 0.7 broadcast_reduce_fusion
  9.5 0.9 fusion.8
  10.3 0.1 broadcast_in_dim.2
  10.5 0.2 copy.11
  10.6 0.2 sqrt_multiply_fusion
  10.8 3.4 multiply_reduce_fusion.1
  14.2 67.8 %all-reduce = (f32[16]{0:T(128)S(1)}, f32[]{:T(128)}) all-reduce(f32[16]{0:T(128)S(1)} %multiply_reduce_fusion.1, f32[]{:T(128)} %broadcast_reduce_fusion), channel_id=1, replica_groups=mesh['ev'=32,'ch'=16] {'ev'}, use_global_device_ids=true, to_apply=%region_1.0 | all-reduce | flops 17 | bytes 136 | tf_op jit(solution)/shard_map/psum | solution.py:11
  81.9 58.2 %all-reduce.5 = (f32[16]{0:T(128)S(1)}, f32[]{:T(128)}) all-reduce(f32[16]{0:T(128)S(1)} %get-tuple-element.10, f32[]{:T(128)} %get-tuple-element.11), channel_id=1, replica_groups=mesh['ev'=32,'ch'=16] {'ch'}, use_global_device_ids=true, to_apply=%region_2.0 | all-reduce | flops 17 | bytes 136 | tf_op jit(solution)/shard_map/psum | solution.py:11
  140.8 0.0 copy-done.2
  140.8 0.0 copy-done
  140.8 0.0 copy-done.1
  140.9 5.4 fusion.4
  146.2 0.0 all-reduce.11.cloned.1.call-update
  146.2 0.0 all-reduce.9.cloned.1.call-start
  146.3 273.8 %all-reduce.11.cloned.1.call-done = (f32[16,4096]{1,0:T(8,128)}, f32[16,4096]{1,0:T(8,128)}) async-done(((f32[16,4096]{1,0:T(8,128)}, f32[16,4096]{1,0:T(8,128)}), (f32[16,4096]{1,0:T(8,128)}, f32[16,4096]{1,0:T(8,128)})) %all-reduce.11.cloned.1.call-update) | async-done | bytes 524304 | tf_op jit(solution)/shard_map/psum | solution.py:38
  420.1 1.2 fusion.7
  421.3 98.8 %all-reduce.4 = (f32[16,16]{1,0:T(8,128)S(1)}, f32[16,16]{1,0:T(8,128)S(1)}, f32[16]{0:T(128)S(1)}) all-reduce(f32[16,16]{1,0:T(8,128)S(1)} %get-tuple-element.9, f32[16,16]{1,0:T(8,128)S(1)} %get-tuple-element.5, f32[16]{0:T(128)S(1)} %get-tuple-element.26), channel_id=1, replica_groups=mesh['ev'=32,'ch'=16] {'ch'}, use_global_device_ids=true, to_apply=%region_9.0 | all-reduce | flops 528 | bytes 4224 | tf_op jit(solution)/shard_map/psum | solution.py:35
  520.1 0.1 broadcast_subtract_fusion.1
  520.2 3.3 multiply_reduce_fusion
  523.5 66.6 %psum.127 = f32[16]{0:T(128)S(1)} all-reduce(f32[16]{0:T(128)S(1)} %multiply_reduce_fusion), channel_id=1, replica_groups=mesh['ev'=32,'ch'=16] {'ev'}, use_global_device_ids=true, to_apply=%region_17.0 | all-reduce | flops 16 | bytes 128 | tf_op jit(solution)/shard_map/psum | solution.py:11
  590.1 46.2 %psum.128 = f32[16]{0:T(128)S(1)} all-reduce(f32[16]{0:T(128)S(1)} %psum.127), channel_id=1, replica_groups=mesh['ev'=32,'ch'=16] {'ch'}, use_global_device_ids=true, to_apply=%region_18.0 | all-reduce | flops 16 | bytes 128 | tf_op jit(solution)/shard_map/psum | solution.py:11
  636.3 5.4 fusion.2
  641.7 0.0 all-reduce.9.cloned.1.call-update
  641.7 273.1 %all-reduce.9.cloned.1.call-done = (f32[16,4096]{1,0:T(8,128)}, f32[16,4096]{1,0:T(8,128)}) async-done(((f32[16,4096]{1,0:T(8,128)}, f32[16,4096]{1,0:T(8,128)}), (f32[16,4096]{1,0:T(8,128)}, f32[16,4096]{1,0:T(8,128)})) %all-reduce.9.cloned.1.call-update) | async-done | bytes 524304 | tf_op jit(solution)/shard_map/psum | solution.py:38
  914.8 1.2 fusion.6
  916.0 98.8 %all-reduce.3 = (f32[16,16]{1,0:T(8,128)S(1)}, f32[16,16]{1,0:T(8,128)S(1)}, f32[16]{0:T(128)S(1)}) all-reduce(f32[16,16]{1,0:T(8,128)S(1)} %get-tuple-element.7, f32[16,16]{1,0:T(8,128)S(1)} %get-tuple-element.3, f32[16]{0:T(128)S(1)} %get-tuple-element.24), channel_id=1, replica_groups=mesh['ev'=32,'ch'=16] {'ch'}, use_global_device_ids=true, to_apply=%region_22.0 | all-reduce | flops 528 | bytes 4224 | tf_op jit(solution)/shard_map/psum | solution.py:35
  1014.8 0.8 broadcast_subtract_fusion
  1015.6 0.6 add_add_fusion
  (5 shorter events, 0.0 us)
Async XLA Ops:
  7.2 133.7 %copy-start.2 = (f32[16]{0:T(128)S(1)}, f32[16]{0:T(128)}, u32[]{:S(2)}) copy-start(f32[16]{0:T(128)} %param.13) | copy-start | bytes 196
  7.2 133.7 %copy-start = (f32[16,4096]{1,0:T(8,128)S(1)}, f32[16,4096]{1,0:T(8,128)}, u32[]{:S(2)}) copy-start(f32[16,4096]{1,0:T(8,128)} %param.10) | copy-start | bytes 786436
  7.2 133.7 %copy-start.1 = (f32[16,16]{1,0:T(8,128)S(1)}, f32[16,16]{1,0:T(8,128)}, u32[]{:S(2)}) copy-start(f32[16,16]{1,0:T(8,128)} %param.9) | copy-start | bytes 3076
  7.2 412.9 %all-reduce.11.cloned.1.call-start = ((), (), s32[]{:S(2)}) async-start(), calls=%async_computation.1 | async-start | bytes 1048576 | tf_op jit(solution)/shard_map/psum | solution.py:38
  146.2 768.5 %all-reduce.9.cloned.1.call-start = ((), (), s32[]{:S(2)}) async-start(), calls=%async_computation | async-start | bytes 1048576 | tf_op jit(solution)/shard_map/psum | solution.py:38
Sparse Core Ops, SparseCore 0:
  146.4 273.6 all-reduce.10
  641.8 272.9 all-reduce.8
